TPU v7x, 32 devices: a whole 2x2x4 slice. The times are simulated.
32 devices in a mesh: groups: 2 (over y), sec: 4 (over z), strip: 4 (over x, core).
Axes of the slice: x: 2, y: 2, z: 4, core: 2. Of those that a mesh axis runs over, the one named last changes fastest.
Arguments:
- sections: bfloat16 [4, 256, 1024], P('sec', 'strip', 'groups'), parts along dimension 2, may hold values from -40 to 40
- mask_fine: int32 [4, 8, 32], P('sec', 'strip', 'groups'), parts along dimension 2, may hold values 0 or 1
- mask_coarse: int32 [4, 4, 16], P('sec', 'strip', 'groups'), parts along dimension 2, may hold values 0 or 1
Outputs:
- corr_fine: float32 [4, 2, 8, 32, 1024], P('sec', None, 'strip', 'groups'), parts along dimension 3
- corr_coarse: float32 [4, 2, 4, 16, 1024], P('sec', None, 'strip', 'groups'), parts along dimension 3
There are 2 independent parts, one for each index of `groups`. A program takes and returns all parts, laid end to end along the dimension named above; each array names one. Nothing has to cross between parts.
All inputs are finite; a program needn't handle non-finite values. No bound on the sum of `mask_fine` or of `mask_coarse` on one device may be relied on, other than what follows from the above.
Results may differ from a plain program's by a relative error of at most 0.0039.
Values may be sent and summed in bfloat16 or wider, within the bound.
A program may use at most 64 MiB of HBM per device.

v0:
```python
import functools

import jax
import jax.numpy as jnp
import numpy as np
from jax import lax
from jax.experimental import pallas as pl
from jax.experimental.pallas import tpu as pltpu
from jax.sharding import PartitionSpec as P

PATCH = 64
STRIDE = 32
WINDOW = 32
HALF = PATCH // 2 + 1
KP = 40
LANES = 128
F32 = jnp.float32
BF16 = jnp.bfloat16


def shifted(value, axis, steps):
    count = lax.axis_size(axis)
    return lax.ppermute(value, axis, [(source, source - steps) for source in range(steps, count)])


def trig(phase):
    angle = 2.0 * np.pi / PATCH * np.mod(phase, PATCH)
    return np.round(np.cos(angle), 12), np.round(np.sin(angle), 12)


def split(table):
    high = np.asarray(table, np.float32).astype(BF16)
    low = (np.asarray(table, np.float64) - high.astype(np.float64)).astype(np.float32).astype(BF16)
    return high, low


def block_diagonal(block, count):
    return np.kron(np.eye(count), block)


def tables(strip_rows):
    fine_rows = strip_rows // STRIDE
    coarse_rows = strip_rows // (2 * STRIDE)
    height = strip_rows + PATCH
    k = np.arange(KP)[:, None]
    keep = (k < HALF).astype(np.float64)
    x = np.arange(height)[None, :]
    units = []
    for i in range(fine_rows):
        c, s = trig(k * (x - STRIDE * i))
        inside = ((x >= STRIDE * i) & (x < STRIDE * i + PATCH)) * keep
        units += [c * inside, -s * inside]
    for i in range(coarse_rows):
        xc = x // 2 - STRIDE * i
        c, s = trig(k * xc)
        inside = ((xc >= 0) & (xc < PATCH)) * keep * 0.25
        units += [c * inside, -s * inside]
    a_high, a_low = split(np.concatenate(units, axis=0))
    first = np.concatenate([a_high, a_low], axis=1)

    freq = np.arange(PATCH)[None, :]
    y = np.arange(STRIDE)[:, None]
    c, s = trig(y * freq)

    def second(c, s, count):
        c, s = block_diagonal(c, count), block_diagonal(s, count)
        return split(np.block([[c, -s], [s, c]]))

    fine_w = second(c, s, LANES // STRIDE)
    coarse_w = second(np.repeat(c, 2, axis=0), np.repeat(s, 2, axis=0), LANES // (2 * STRIDE))

    shift = np.arange(WINDOW) - WINDOW // 2
    c, s = trig(np.arange(PATCH)[:, None] * shift[None, :])
    c, s = block_diagonal(c, 4), block_diagonal(s, 4)
    inverse = split(np.block([[c, s], [-s, c]]))

    weight = np.where((k == 0) | (k == PATCH // 2), 1.0, 2.0) * keep
    c, s = trig(shift[:, None] * np.arange(KP)[None, :])
    last_high, last_low = split(np.concatenate([c * weight.T, -s * weight.T], axis=1))
    last = np.concatenate([last_high, last_high, last_low], axis=1)
    energy = np.kron(np.eye(4), np.ones((PATCH, WINDOW)))
    return [
        first,
        *fine_w,
        *coarse_w,
        *inverse,
        last,
        np.asarray(energy, np.float32),
        np.asarray(np.broadcast_to(weight, (KP, LANES)), np.float32),
    ]


def split_value(value):
    high = value.astype(BF16)
    return high, (value - high.astype(F32)).astype(BF16)


def matmul(a, b):
    return jnp.dot(a, b, preferred_element_type=F32)


def section_spectra(pixels, first, fine_w, coarse_w, fine_rows, coarse_rows):
    half = matmul(first, jnp.concatenate([pixels, pixels], axis=0))
    width = half.shape[1]
    tiles = width // LANES
    row = lax.broadcasted_iota(jnp.int32, (KP, width), 0)
    fine_in, coarse_in = [], []
    for unit in range(fine_rows + coarse_rows):
        real = half[2 * KP * unit : 2 * KP * unit + KP]
        imag = half[2 * KP * unit + KP : 2 * KP * (unit + 1)]
        sums = real[0:1]
        high = sums.astype(BF16).astype(F32)
        middle = (sums - high).astype(BF16).astype(F32)
        low = sums - high - middle
        real = jnp.where(row == 0, high, real)
        real = jnp.where(row == HALF, middle, real)
        real = jnp.where(row == HALF + 1, low, real)
        target = fine_in if unit < fine_rows else coarse_in
        for tile in range(tiles):
            at = slice(LANES * tile, LANES * (tile + 1))
            target.append(jnp.concatenate([real[:, at], imag[:, at]], axis=1))

    def transform(parts, weights):
        high, low = split_value(jnp.concatenate(parts, axis=0))
        w_high, w_low = weights
        return matmul(high, w_high) + matmul(low, w_high) + matmul(high, w_low)

    fine = transform(fine_in, fine_w)
    coarse = transform(coarse_in, coarse_w)
    wide = 2 * LANES
    lane = lax.broadcasted_iota(jnp.int32, (KP, wide), 1)
    krow = lax.broadcasted_iota(jnp.int32, (KP, wide), 0)
    sign = jnp.where(lane % 2 == 0, 1.0, -1.0).astype(F32)
    dc = (krow == 0) & (lane % PATCH == 0)

    def finish(parts, rows):
        count = len(parts) // rows
        rolled = [pltpu.roll(part, wide - PATCH, 1) for part in parts]
        done = []
        for index, part in enumerate(parts):
            if index % count == count - 1:
                following = jnp.where(lane < wide - PATCH, rolled[index], 0.0)
            else:
                following = jnp.where(lane < wide - PATCH, rolled[index], rolled[index + 1])
            value = part + sign * following
            value = jnp.where(krow == 0, value + value[HALF : HALF + 1] + value[HALF + 1 : HALF + 2], value)
            value = jnp.where(dc, 0.0, value)
            done.append(value)
        return done

    def groups(offset):
        fine_parts = [
            fine[KP * g : KP * (g + 1), offset * wide : (offset + 1) * wide]
            for g in range(fine_rows * tiles)
        ]
        coarse_parts = [
            jnp.concatenate(
                [
                    coarse[KP * g : KP * (g + 1), offset * LANES : (offset + 1) * LANES],
                    coarse[KP * (g + 1) : KP * (g + 2), offset * LANES : (offset + 1) * LANES],
                ],
                axis=1,
            )
            for g in range(0, coarse_rows * tiles, 2)
        ]
        return finish(fine_parts, fine_rows) + finish(coarse_parts, coarse_rows)

    return groups(0), groups(1)


def block_transpose(value):
    row = lax.broadcasted_iota(jnp.int32, value.shape, 0) % 4
    block = lax.broadcasted_iota(jnp.int32, value.shape, 1) // WINDOW
    rows = value.shape[0]
    moved = pltpu.roll(value, 2 * WINDOW, 1)
    other = jnp.where(row < 2, pltpu.roll(moved, rows - 2, 0), pltpu.roll(moved, 2, 0))
    value = jnp.where((row // 2) == (block // 2), value, other)
    right = pltpu.roll(pltpu.roll(value, WINDOW, 1), rows - 1, 0)
    left = pltpu.roll(pltpu.roll(value, LANES - WINDOW, 1), 1, 0)
    other = jnp.where(row % 2 == 0, right, left)
    return jnp.where((row % 2) == (block % 2), value, other)


def compute(
    pixels_ref,
    fine_mask_ref,
    coarse_mask_ref,
    first_ref,
    fine_high_ref,
    fine_low_ref,
    coarse_high_ref,
    coarse_low_ref,
    inverse_high_ref,
    inverse_low_ref,
    last_ref,
    energy_ref,
    weight_ref,
    fine_out_ref,
    coarse_out_ref,
    real_ref,
    imag_ref,
    sums_ref,
):
    fine_rows, fine_cols = fine_mask_ref.shape[1:]
    coarse_rows, coarse_cols = coarse_mask_ref.shape[1:]
    count = (fine_rows * fine_cols + coarse_rows * coarse_cols) // 4
    fine_groups = fine_rows * fine_cols // 4
    weight = jnp.concatenate([weight_ref[...]] * 2, axis=1)
    for section in range(3):
        real, imag = section_spectra(
            pixels_ref[section],
            first_ref[...],
            (fine_high_ref[...], fine_low_ref[...]),
            (coarse_high_ref[...], coarse_low_ref[...]),
            fine_rows,
            coarse_rows,
        )
        for g in range(count):
            real_ref[section, KP * g : KP * (g + 1)] = real[g]
            imag_ref[section, KP * g : KP * (g + 1)] = imag[g]
            power = weight * (real[g] * real[g] + imag[g] * imag[g])
            sums_ref[section, g : g + 1] = jnp.sum(power, axis=0, keepdims=True)
    scales = []
    for section in range(3):
        total = jnp.dot(
            sums_ref[section], energy_ref[...], preferred_element_type=F32, precision=lax.Precision.HIGHEST
        )
        scales.append(1.0 / jnp.sqrt(total * (1.0 / float(PATCH) ** 4) + 1e-05))

    def spread(mask, cols):
        source = lax.broadcasted_iota(jnp.int32, (cols, cols * WINDOW), 0)
        target = lax.broadcasted_iota(jnp.int32, (cols, cols * WINDOW), 1) // WINDOW
        picks = jnp.where(source == target, 1.0, 0.0).astype(BF16)
        return matmul(mask.astype(F32).astype(BF16), picks)

    fine_mask = spread(fine_mask_ref[0], fine_cols)
    coarse_mask = spread(coarse_mask_ref[0], coarse_cols)
    masks = [
        m[r : r + 1, LANES * t : LANES * (t + 1)]
        for m in (fine_mask, coarse_mask)
        for r in range(m.shape[0])
        for t in range(m.shape[1] // LANES)
    ]
    stacked = []
    for d in (1, 2):
        cross_real = real_ref[0] * real_ref[d] + imag_ref[0] * imag_ref[d]
        cross_imag = real_ref[0] * imag_ref[d] - imag_ref[0] * real_ref[d]
        cross = jnp.concatenate([cross_real.astype(BF16), cross_imag.astype(BF16)], axis=1)
        rows = matmul(cross, inverse_high_ref[...]) + matmul(cross, inverse_low_ref[...])
        for g in range(count):
            part = rows[KP * g : KP * (g + 1)]
            stacked.append(jnp.concatenate([part[:, :LANES], part[:, LANES:]], axis=0))
    high, low = split_value(jnp.concatenate(stacked, axis=1))
    maps = matmul(last_ref[...], jnp.concatenate([high, low, high], axis=0))
    for d in (1, 2):
        for g in range(count):
            scale = scales[0][g : g + 1] * scales[d][g : g + 1] * masks[g] * (1.0 / float(PATCH) ** 3)
            at = LANES * (count * (d - 1) + g)
            value = block_transpose(maps[:, at : at + LANES] * scale)
            if g < fine_groups:
                ref, local_g, cols = fine_out_ref, g, fine_cols
            else:
                ref, local_g, cols = coarse_out_ref, g - fine_groups, coarse_cols
            i, j = divmod(4 * local_g, cols)
            for q in range(WINDOW // 4):
                ref[0, d - 1, i, j : j + 4, LANES * q : LANES * (q + 1)] = value[4 * q : 4 * (q + 1)]


def local(sections, mask_fine, mask_coarse):
    strip_rows = sections.shape[1]
    near = shifted(sections, "sec", 1)
    far = shifted(sections, "sec", 2)
    own = jnp.concatenate([sections, near, far], axis=0)
    rim = shifted(own, "strip", 1)
    pixels = jnp.concatenate([own, rim], axis=1)
    consts = [jnp.asarray(t) for t in tables(strip_rows)]
    fine_rows, fine_cols = mask_fine.shape[1:]
    coarse_rows, coarse_cols = mask_coarse.shape[1:]
    count = (fine_rows * fine_cols + coarse_rows * coarse_cols) // 4
    vmem = pl.BlockSpec(memory_space=pltpu.VMEM)
    flat = WINDOW * WINDOW
    return pl.pallas_call(
        compute,
        out_shape=(
            jax.ShapeDtypeStruct((1, 2, fine_rows, fine_cols, flat), F32),
            jax.ShapeDtypeStruct((1, 2, coarse_rows, coarse_cols, flat), F32),
        ),
        in_specs=[vmem] * (3 + len(consts)),
        out_specs=(vmem, vmem),
        scratch_shapes=[
            pltpu.VMEM((3, KP * count, 2 * LANES), F32),
            pltpu.VMEM((3, KP * count, 2 * LANES), F32),
            pltpu.VMEM((3, -(-count // 8) * 8, 2 * LANES), F32),
        ],
    )(pixels, mask_fine, mask_coarse, *consts)


def solution(mesh):
    in_specs = (
        P("sec", "strip", "groups"),
        P("sec", "strip", "groups"),
        P("sec", "strip", "groups"),
    )
    out_specs = (P("sec", None, "strip", "groups", None), P("sec", None, "strip", "groups", None))
    return jax.shard_map(local, mesh=mesh, in_specs=in_specs, out_specs=out_specs, check_vma=False)
```

profile of v0, /device:TPU:1, one launch (start us, length us, event | category | flops | bytes accessed | tf_op | source)
XLA Modules:
  0.0 23.9 jit_solution(9382061455991766576)
XLA Ops:
  0.6 1.3 %collective-permute-start = (bf16[1,64,512]{2,1,0:T(8,128)(2,1)}, bf16[1,64,512]{2,1,0:T(8,128)(2,1)S(1)}, u32[]{:S(2)}, u32[]{:S(2)}) collective-permute-start(bf16[1,64,512]{2,1,0:T(8,128)(2,1)} %param.13), channel_id=1, source_target_pairs={{4,0},{8,4},{12,8},{5,1},{9,5},{13,9},{6,2},{10,6},{14,10},{7,3},{... | collective-permute-start | bytes 196616 | tf_op jit(solution)/shard_map/ppermute | solution.py:23
  1.9 1.3 %collective-permute-start.1 = (bf16[1,64,512]{2,1,0:T(8,128)(2,1)}, bf16[1,64,512]{2,1,0:T(8,128)(2,1)S(1)}, u32[]{:S(2)}, u32[]{:S(2)}) collective-permute-start(bf16[1,64,512]{2,1,0:T(8,128)(2,1)} %param.13), channel_id=1, source_target_pairs={{8,0},{12,4},{9,1},{13,5},{10,2},{14,6},{11,3},{15,7},{24,16},{28,... | collective-permute-start | bytes 196616 | tf_op jit(solution)/shard_map/ppermute | solution.py:23
  3.2 0.8 %constant_dynamic-update-slice_fusion.2 = bf16[3,64,512]{2,1,0:T(8,128)(2,1)S(1)} fusion(bf16[1,64,512]{2,1,0:T(8,128)(2,1)} %param.13), kind=kLoop, calls=%fused_computation.3 | loop fusion | bytes 131072
  4.1 2.4 %collective-permute-done = bf16[1,64,512]{2,1,0:T(8,128)(2,1)S(1)} collective-permute-done((bf16[1,64,512]{2,1,0:T(8,128)(2,1)}, bf16[1,64,512]{2,1,0:T(8,128)(2,1)S(1)}, u32[]{:S(2)}, u32[]{:S(2)}) %collective-permute-start) | collective-permute-done | bytes 65568 | tf_op jit(solution)/shard_map/ppermute | solution.py:23
  6.5 3.4 %collective-permute-done.1 = bf16[1,64,512]{2,1,0:T(8,128)(2,1)S(1)} collective-permute-done((bf16[1,64,512]{2,1,0:T(8,128)(2,1)}, bf16[1,64,512]{2,1,0:T(8,128)(2,1)S(1)}, u32[]{:S(2)}, u32[]{:S(2)}) %collective-permute-start.1) | collective-permute-done | bytes 65568 | tf_op jit(solution)/shard_map/ppermute | solution.py:23
  9.9 3.6 %collective-permute-start.2 = (bf16[3,64,512]{2,1,0:T(8,128)(2,1)S(1)}, bf16[3,64,512]{2,1,0:T(8,128)(2,1)S(1)}, u32[]{:S(2)}, u32[]{:S(2)}) collective-permute-start(bf16[3,64,512]{2,1,0:T(8,128)(2,1)S(1)} %constant_dynamic-update-slice_fusion), channel_id=1, source_target_pairs={{1,0},{2,1},{3,2},{5,4},{6,5},{7,6},{9,8},{10,9},{11,10},{13,12},{... | collective-permute-start | bytes 589832 | tf_op jit(solution)/shard_map/ppermute | solution.py:23
  13.5 4.4 %collective-permute-done.2 = bf16[3,64,512]{2,1,0:T(8,128)(2,1)S(1)} collective-permute-done((bf16[3,64,512]{2,1,0:T(8,128)(2,1)S(1)}, bf16[3,64,512]{2,1,0:T(8,128)(2,1)S(1)}, u32[]{:S(2)}, u32[]{:S(2)}) %collective-permute-start.2) | collective-permute-done | bytes 196640 | tf_op jit(solution)/shard_map/ppermute | solution.py:23
  18.0 0.8 %pad_maximum_fusion.pixels_ref = bf16[3,128,512]{2,1,0:T(8,128)(2,1)} fusion(bf16[3,64,512]{2,1,0:T(8,128)(2,1)S(1)} %collective-permute-done.2, bf16[3,64,512]{2,1,0:T(8,128)(2,1)S(1)} %constant_dynamic-update-slice_fusion), kind=kLoop, calls=%fused_computation | loop fusion | flops 786432 | bytes 786432 | tf_op jit(solution)/shard_map/concatenate | solution.py:275
  18.7 5.2 %shard_map.140 = (f32[1,2,2,16,1024]{4,3,2,1,0:T(8,128)}, f32[1,2,1,8,1024]{4,3,2,1,0:T(8,128)}) custom-call(bf16[3,128,512]{2,1,0:T(8,128)(2,1)} %pad_maximum_fusion.pixels_ref, s32[1,2,16]{2,1,0:T(2,128)} %fine_mask_ref.1, s32[1,1,8]{2,1,0:T(1,128)} %coarse_mask_ref.1, bf16[240,256]{1,0:T(8,128)(2,1)} %constant.20.clone.first_ref, ...), custom_call_target="tpu_custom_call" | custom-call | tf_op jit(solution)/shard_map/pallas_call | solution.py:282
  (2 shorter events, 0.0 us)
Async XLA Ops:
  0.6 5.9 %collective-permute-start = (bf16[1,64,512]{2,1,0:T(8,128)(2,1)}, bf16[1,64,512]{2,1,0:T(8,128)(2,1)S(1)}, u32[]{:S(2)}, u32[]{:S(2)}) collective-permute-start(bf16[1,64,512]{2,1,0:T(8,128)(2,1)} %param.13), channel_id=1, source_target_pairs={{4,0},{8,4},{12,8},{5,1},{9,5},{13,9},{6,2},{10,6},{14,10},{7,3},{... | collective-permute-start | bytes 196616 | tf_op jit(solution)/shard_map/ppermute | solution.py:23
  1.9 8.0 %collective-permute-start.1 = (bf16[1,64,512]{2,1,0:T(8,128)(2,1)}, bf16[1,64,512]{2,1,0:T(8,128)(2,1)S(1)}, u32[]{:S(2)}, u32[]{:S(2)}) collective-permute-start(bf16[1,64,512]{2,1,0:T(8,128)(2,1)} %param.13), channel_id=1, source_target_pairs={{8,0},{12,4},{9,1},{13,5},{10,2},{14,6},{11,3},{15,7},{24,16},{28,... | collective-permute-start | bytes 196616 | tf_op jit(solution)/shard_map/ppermute | solution.py:23
  9.9 8.0 %collective-permute-start.2 = (bf16[3,64,512]{2,1,0:T(8,128)(2,1)S(1)}, bf16[3,64,512]{2,1,0:T(8,128)(2,1)S(1)}, u32[]{:S(2)}, u32[]{:S(2)}) collective-permute-start(bf16[3,64,512]{2,1,0:T(8,128)(2,1)S(1)} %constant_dynamic-update-slice_fusion), channel_id=1, source_target_pairs={{1,0},{2,1},{3,2},{5,4},{6,5},{7,6},{9,8},{10,9},{11,10},{13,12},{... | collective-permute-start | bytes 589832 | tf_op jit(solution)/shard_map/ppermute | solution.py:23
where the time goes:
time: 24.2 us; the launch traced here: 23.9 us
  waiting for transfers between devices  10.3 us (43%)
  starting transfers between devices  6.18 us (26%)
  Pallas kernels  5.18 us (21%)
  local copies, waits for them, and re-layouts  0.86 us (4%)
  other arithmetic  0.78 us (3%)
  between operations  0.66 us (3%)
    ppermute x3, waiting for transfers between devices, shifted(): lax.ppermute(value, axis, [(source, source - steps) for source in range(s...  10.3 us
    ppermute x3, starting transfers between devices, shifted(): lax.ppermute(value, axis, [(source, source - steps) for source in range(s...  6.18 us
    pallas_call x1, Pallas kernels, local(): pl.pallas_call(compute, out_shape=(jax.ShapeDtypeStruct((1, 2, fine_rows,...  5.18 us
    unnamed x2, local copies, waits for them, and re-layouts  0.85 us
    concatenate x1, other arithmetic, local(): pixels = jnp.concatenate([own, rim], axis=1)  0.78 us
  transfers between devices with their start and end apart: 3, of which 3 were waited for; matrix products, arithmetic and copies ran while one was open for 4% of the time, Pallas kernels for 0%

commit v1 on v0

--- a/solution.py
+++ b/solution.py
@@ -16,11 +16,7 @@
 LANES = 128
 F32 = jnp.float32
 BF16 = jnp.bfloat16
-
-
-def shifted(value, axis, steps):
-    count = lax.axis_size(axis)
-    return lax.ppermute(value, axis, [(source, source - steps) for source in range(steps, count)])
+MESH = pl.DeviceIdType.MESH
 
 
 def trig(phase):
@@ -181,34 +177,112 @@
     return jnp.where((row % 2) == (block % 2), value, other)
 
 
-def compute(
-    pixels_ref,
-    fine_mask_ref,
-    coarse_mask_ref,
-    first_ref,
-    fine_high_ref,
-    fine_low_ref,
-    coarse_high_ref,
-    coarse_low_ref,
-    inverse_high_ref,
-    inverse_low_ref,
-    last_ref,
-    energy_ref,
-    weight_ref,
-    fine_out_ref,
-    coarse_out_ref,
-    real_ref,
-    imag_ref,
-    sums_ref,
-):
+def compute(const_count, *refs):
+    pixels_ref, fine_mask_ref, coarse_mask_ref = refs[:3]
+    sources = refs[3 : 3 + const_count]
+    fine_out_ref, coarse_out_ref = refs[3 + const_count : 5 + const_count]
+    own_ref, near_ref, far_ref, rim_ref, real_ref, imag_ref, sums_ref = refs[5 + const_count : 12 + const_count]
+    held = refs[12 + const_count : 12 + 2 * const_count]
+    own_sem, const_sem, send_sem, recv_sem = refs[12 + 2 * const_count :]
+    sec, strip = lax.axis_index("sec"), lax.axis_index("strip")
+    secs, strips = lax.axis_size("sec"), lax.axis_size("strip")
+
+    own_copy = pltpu.make_async_copy(pixels_ref.at[0], own_ref, own_sem)
+    own_copy.start()
+    const_copies = [
+        pltpu.make_async_copy(source, target, const_sem.at[index])
+        for index, (source, target) in enumerate(zip(sources, held))
+    ]
+    for copy in const_copies:
+        copy.start()
+
+    barrier = pltpu.get_barrier_semaphore()
+
+    def greet(condition, device):
+        @pl.when(condition)
+        def _():
+            pl.semaphore_signal(barrier, inc=1, device_id=device, device_id_type=MESH)
+
+    greet(sec + 2 < secs, {"sec": sec + 2})
+    greet(sec + 1 < secs, {"sec": sec + 1})
+    greet(strip + 1 < strips, {"strip": strip + 1})
+    targets = lax.min(sec, 2) + lax.min(strip, 1)
+
+    @pl.when(targets >= 1)
+    def _():
+        pl.semaphore_wait(barrier, targets)
+
+    def remote(source, target, index, device):
+        return pltpu.make_async_remote_copy(
+            src_ref=source,
+            dst_ref=target,
+            send_sem=send_sem.at[index],
+            recv_sem=recv_sem.at[index],
+            device_id=device,
+            device_id_type=MESH,
+        )
+
+    far_copy = remote(pixels_ref.at[0], far_ref, 0, {"sec": sec - 2})
+    near_copy = remote(pixels_ref.at[0], near_ref, 1, {"sec": sec - 1})
+    rim_copies = [
+        remote(source, rim_ref.at[index], 2 + index, {"strip": strip - 1})
+        for index, source in enumerate((pixels_ref.at[0], near_ref, far_ref))
+    ]
+    up = strip >= 1
+    below = strip + 1 < strips
+    pl.when(sec >= 2)(far_copy.start)
+    pl.when(sec >= 1)(near_copy.start)
+    pl.when(up)(rim_copies[0].start)
+
+    def fill(condition, ref, *index):
+        @pl.when(condition)
+        def _():
+            ref[index if index else ...] = jnp.zeros(ref.shape[len(index) :], ref.dtype)
+
+    for d in range(3):
+        fill(jnp.logical_not(below & (sec + d < secs)), rim_ref, d)
+    fill(sec + 1 >= secs, near_ref)
+    fill(sec + 2 >= secs, far_ref)
+    sums_ref[...] = jnp.zeros_like(sums_ref)
+
     fine_rows, fine_cols = fine_mask_ref.shape[1:]
     coarse_rows, coarse_cols = coarse_mask_ref.shape[1:]
     count = (fine_rows * fine_cols + coarse_rows * coarse_cols) // 4
     fine_groups = fine_rows * fine_cols // 4
-    weight = jnp.concatenate([weight_ref[...]] * 2, axis=1)
-    for section in range(3):
+    (
+        first_ref,
+        fine_high_ref,
+        fine_low_ref,
+        coarse_high_ref,
+        coarse_low_ref,
+        inverse_high_ref,
+        inverse_low_ref,
+        last_ref,
+        energy_ref,
+        weight_ref,
+    ) = held
+
+    def spread(mask, cols):
+        source = lax.broadcasted_iota(jnp.int32, (cols, cols * WINDOW), 0)
+        target = lax.broadcasted_iota(jnp.int32, (cols, cols * WINDOW), 1) // WINDOW
+        picks = jnp.where(source == target, 1.0, 0.0).astype(BF16)
+        return matmul(mask.astype(F32).astype(BF16), picks)
+
+    fine_mask = spread(fine_mask_ref[0], fine_cols)
+    coarse_mask = spread(coarse_mask_ref[0], coarse_cols)
+    masks = [
+        m[r : r + 1, LANES * t : LANES * (t + 1)]
+        for m in (fine_mask, coarse_mask)
+        for r in range(m.shape[0])
+        for t in range(m.shape[1] // LANES)
+    ]
+    scales = []
+
+    def analyse(section, main_ref):
+        pl.when(below & (sec + section < secs))(rim_copies[section].wait_recv)
+        weight = jnp.concatenate([weight_ref[...]] * 2, axis=1)
         real, imag = section_spectra(
-            pixels_ref[section],
+            jnp.concatenate([main_ref[...], rim_ref[section]], axis=0),
             first_ref[...],
             (fine_high_ref[...], fine_low_ref[...]),
             (coarse_high_ref[...], coarse_low_ref[...]),
@@ -220,43 +294,25 @@
             imag_ref[section, KP * g : KP * (g + 1)] = imag[g]
             power = weight * (real[g] * real[g] + imag[g] * imag[g])
             sums_ref[section, g : g + 1] = jnp.sum(power, axis=0, keepdims=True)
-    scales = []
-    for section in range(3):
         total = jnp.dot(
             sums_ref[section], energy_ref[...], preferred_element_type=F32, precision=lax.Precision.HIGHEST
         )
         scales.append(1.0 / jnp.sqrt(total * (1.0 / float(PATCH) ** 4) + 1e-05))
 
-    def spread(mask, cols):
-        source = lax.broadcasted_iota(jnp.int32, (cols, cols * WINDOW), 0)
-        target = lax.broadcasted_iota(jnp.int32, (cols, cols * WINDOW), 1) // WINDOW
-        picks = jnp.where(source == target, 1.0, 0.0).astype(BF16)
-        return matmul(mask.astype(F32).astype(BF16), picks)
-
-    fine_mask = spread(fine_mask_ref[0], fine_cols)
-    coarse_mask = spread(coarse_mask_ref[0], coarse_cols)
-    masks = [
-        m[r : r + 1, LANES * t : LANES * (t + 1)]
-        for m in (fine_mask, coarse_mask)
-        for r in range(m.shape[0])
-        for t in range(m.shape[1] // LANES)
-    ]
-    stacked = []
-    for d in (1, 2):
+    def correlate(d):
         cross_real = real_ref[0] * real_ref[d] + imag_ref[0] * imag_ref[d]
         cross_imag = real_ref[0] * imag_ref[d] - imag_ref[0] * real_ref[d]
         cross = jnp.concatenate([cross_real.astype(BF16), cross_imag.astype(BF16)], axis=1)
         rows = matmul(cross, inverse_high_ref[...]) + matmul(cross, inverse_low_ref[...])
+        stacked = []
         for g in range(count):
             part = rows[KP * g : KP * (g + 1)]
             stacked.append(jnp.concatenate([part[:, :LANES], part[:, LANES:]], axis=0))
-    high, low = split_value(jnp.concatenate(stacked, axis=1))
-    maps = matmul(last_ref[...], jnp.concatenate([high, low, high], axis=0))
-    for d in (1, 2):
+        high, low = split_value(jnp.concatenate(stacked, axis=1))
+        maps = matmul(last_ref[...], jnp.concatenate([high, low, high], axis=0))
         for g in range(count):
             scale = scales[0][g : g + 1] * scales[d][g : g + 1] * masks[g] * (1.0 / float(PATCH) ** 3)
-            at = LANES * (count * (d - 1) + g)
-            value = block_transpose(maps[:, at : at + LANES] * scale)
+            value = block_transpose(maps[:, LANES * g : LANES * (g + 1)] * scale)
             if g < fine_groups:
                 ref, local_g, cols = fine_out_ref, g, fine_cols
             else:
@@ -265,34 +321,59 @@
             for q in range(WINDOW // 4):
                 ref[0, d - 1, i, j : j + 4, LANES * q : LANES * (q + 1)] = value[4 * q : 4 * (q + 1)]
 
+    own_copy.wait()
+    for copy in const_copies:
+        copy.wait()
+    has_near, has_far = sec + 1 < secs, sec + 2 < secs
+    pl.when(has_near)(near_copy.wait_recv)
+    pl.when(has_near & up)(rim_copies[1].start)
+    analyse(0, own_ref)
+    pl.when(has_far)(far_copy.wait_recv)
+    pl.when(has_far & up)(rim_copies[2].start)
+    analyse(1, near_ref)
+    correlate(1)
+    analyse(2, far_ref)
+    correlate(2)
+    pl.when(sec >= 2)(far_copy.wait_send)
+    pl.when(sec >= 1)(near_copy.wait_send)
+    pl.when(up)(rim_copies[0].wait_send)
+    pl.when(has_near & up)(rim_copies[1].wait_send)
+    pl.when(has_far & up)(rim_copies[2].wait_send)
+
 
 def local(sections, mask_fine, mask_coarse):
-    strip_rows = sections.shape[1]
-    near = shifted(sections, "sec", 1)
-    far = shifted(sections, "sec", 2)
-    own = jnp.concatenate([sections, near, far], axis=0)
-    rim = shifted(own, "strip", 1)
-    pixels = jnp.concatenate([own, rim], axis=1)
+    strip_rows, width = sections.shape[1:]
     consts = [jnp.asarray(t) for t in tables(strip_rows)]
     fine_rows, fine_cols = mask_fine.shape[1:]
     coarse_rows, coarse_cols = mask_coarse.shape[1:]
     count = (fine_rows * fine_cols + coarse_rows * coarse_cols) // 4
     vmem = pl.BlockSpec(memory_space=pltpu.VMEM)
+    anywhere = pl.BlockSpec(memory_space=pl.ANY)
     flat = WINDOW * WINDOW
     return pl.pallas_call(
-        compute,
+        functools.partial(compute, len(consts)),
         out_shape=(
             jax.ShapeDtypeStruct((1, 2, fine_rows, fine_cols, flat), F32),
             jax.ShapeDtypeStruct((1, 2, coarse_rows, coarse_cols, flat), F32),
         ),
-        in_specs=[vmem] * (3 + len(consts)),
+        in_specs=[anywhere, vmem, vmem] + [anywhere] * len(consts),
         out_specs=(vmem, vmem),
         scratch_shapes=[
+            pltpu.VMEM((strip_rows, width), BF16),
+            pltpu.VMEM((strip_rows, width), BF16),
+            pltpu.VMEM((strip_rows, width), BF16),
+            pltpu.VMEM((3, strip_rows, width), BF16),
             pltpu.VMEM((3, KP * count, 2 * LANES), F32),
             pltpu.VMEM((3, KP * count, 2 * LANES), F32),
             pltpu.VMEM((3, -(-count // 8) * 8, 2 * LANES), F32),
+            *[pltpu.VMEM(c.shape, c.dtype) for c in consts],
+            pltpu.SemaphoreType.DMA,
+            pltpu.SemaphoreType.DMA((len(consts),)),
+            pltpu.SemaphoreType.DMA((5,)),
+            pltpu.SemaphoreType.DMA((5,)),
         ],
-    )(pixels, mask_fine, mask_coarse, *consts)
+        compiler_params=pltpu.CompilerParams(collective_id=0, has_side_effects=True),
+    )(sections, mask_fine, mask_coarse, *consts)
 
 
 def solution(mesh):

time: 24.2 us -> 19.6 us (0.81)
  the two profiles are of different devices: /device:TPU:1 before, /device:TPU:9 now
where the time goes in v1:
time: 19.6 us; the launch traced here: 19.4 us
  Pallas kernels  16.4 us (84%)
  local copies, waits for them, and re-layouts  2.34 us (12%)
  between operations  0.65 us (3%)
    pallas_call x1, Pallas kernels, local(): pl.pallas_call(functools.partial(compute, len(consts)), out_shape=(jax.Sh...  16.4 us
    unnamed x4, local copies, waits for them, and re-layouts  2.34 us

profile of v1, /device:TPU:9, one launch (start us, length us, event | category | flops | bytes accessed | tf_op | source)
XLA Modules:
  0.0 19.4 jit_solution(9877939406993601705)
XLA Ops:
  0.6 16.4 %shard_map.140 = (f32[1,2,2,16,1024]{4,3,2,1,0:T(8,128)}, f32[1,2,1,8,1024]{4,3,2,1,0:T(8,128)}) custom-call(bf16[1,64,512]{2,1,0:T(8,128)(2,1)} %refs_0_.1, s32[1,2,16]{2,1,0:T(2,128)} %refs_1_.1, s32[1,1,8]{2,1,0:T(1,128)} %refs_2_.1, bf16[240,256]{1,0:T(8,128)(2,1)} %constant.20.clone.refs_3_, bf16[256,512]{1,0:T(8,128)(2,1)} %constant.21.clone.refs_4_, ...), custom_call_target="tpu_custom_call" | custom-call | tf_op jit(solution)/shard_map/pallas_call | solution.py:353
  17.1 0.0 copy-start
  17.1 1.7 %copy.17 = f32[1,2,2,16,1024]{4,3,2,1,0:T(8,128)} copy(f32[1,2,2,16,1024]{4,3,2,1,0:T(8,128)} %get-tuple-element.4) | data formatting | bytes 524288
  18.8 0.0 copy-done
  18.8 0.6 %copy.18 = f32[1,2,1,8,1024]{4,3,2,1,0:T(8,128)} copy(f32[1,2,1,8,1024]{4,3,2,1,0:T(8,128)S(1)} %copy-done) | data formatting | bytes 131072
Async XLA Ops:
  17.1 1.7 %copy-start = (f32[1,2,1,8,1024]{4,3,2,1,0:T(8,128)S(1)}, f32[1,2,1,8,1024]{4,3,2,1,0:T(8,128)}, u32[]{:S(2)}) copy-start(f32[1,2,1,8,1024]{4,3,2,1,0:T(8,128)} %get-tuple-element.5) | copy-start | bytes 196612

commit v2 on v1

--- a/solution.py
+++ b/solution.py
@@ -13,6 +13,7 @@
 WINDOW = 32
 HALF = PATCH // 2 + 1
 KP = 40
+CHUNKS = 2
 LANES = 128
 F32 = jnp.float32
 BF16 = jnp.bfloat16
@@ -180,10 +181,10 @@
 def compute(const_count, *refs):
     pixels_ref, fine_mask_ref, coarse_mask_ref = refs[:3]
     sources = refs[3 : 3 + const_count]
-    fine_out_ref, coarse_out_ref = refs[3 + const_count : 5 + const_count]
-    own_ref, near_ref, far_ref, rim_ref, real_ref, imag_ref, sums_ref = refs[5 + const_count : 12 + const_count]
-    held = refs[12 + const_count : 12 + 2 * const_count]
-    own_sem, const_sem, send_sem, recv_sem = refs[12 + 2 * const_count :]
+    maps_ref = refs[3 + const_count]
+    own_ref, near_ref, far_ref, rim_ref, real_ref, imag_ref, sums_ref = refs[4 + const_count : 11 + const_count]
+    held = refs[11 + const_count : 11 + 2 * const_count]
+    own_sem, const_sem, send_sem, recv_sem = refs[11 + 2 * const_count :]
     sec, strip = lax.axis_index("sec"), lax.axis_index("strip")
     secs, strips = lax.axis_size("sec"), lax.axis_size("strip")
 
@@ -203,36 +204,46 @@
         def _():
             pl.semaphore_signal(barrier, inc=1, device_id=device, device_id_type=MESH)
 
-    greet(sec + 2 < secs, {"sec": sec + 2})
     greet(sec + 1 < secs, {"sec": sec + 1})
     greet(strip + 1 < strips, {"strip": strip + 1})
-    targets = lax.min(sec, 2) + lax.min(strip, 1)
+    targets = lax.min(sec, 1) + lax.min(strip, 1)
 
     @pl.when(targets >= 1)
     def _():
         pl.semaphore_wait(barrier, targets)
 
-    def remote(source, target, index, device):
+    piece = pixels_ref.shape[1] // CHUNKS
+
+    def remote(source, target, flow, chunk, device):
+        rows = pl.ds(piece * chunk, piece)
         return pltpu.make_async_remote_copy(
-            src_ref=source,
-            dst_ref=target,
-            send_sem=send_sem.at[index],
-            recv_sem=recv_sem.at[index],
+            src_ref=source.at[rows],
+            dst_ref=target.at[rows],
+            send_sem=send_sem.at[flow, chunk],
+            recv_sem=recv_sem.at[flow, chunk],
             device_id=device,
             device_id_type=MESH,
         )
 
-    far_copy = remote(pixels_ref.at[0], far_ref, 0, {"sec": sec - 2})
-    near_copy = remote(pixels_ref.at[0], near_ref, 1, {"sec": sec - 1})
+    above, before = {"strip": strip - 1}, {"sec": sec - 1}
     rim_copies = [
-        remote(source, rim_ref.at[index], 2 + index, {"strip": strip - 1})
+        [remote(source, rim_ref.at[index], index, c, above) for c in range(CHUNKS)]
         for index, source in enumerate((pixels_ref.at[0], near_ref, far_ref))
     ]
+    near_copies = [remote(pixels_ref.at[0], near_ref, 3, c, before) for c in range(CHUNKS)]
+    far_copies = [remote(near_ref, far_ref, 4, c, before) for c in range(CHUNKS)]
     up = strip >= 1
     below = strip + 1 < strips
-    pl.when(sec >= 2)(far_copy.start)
-    pl.when(sec >= 1)(near_copy.start)
-    pl.when(up)(rim_copies[0].start)
+    has_near, has_far = sec + 1 < secs, sec + 2 < secs
+
+    def each(condition, copies, method):
+        @pl.when(condition)
+        def _():
+            for copy in copies:
+                getattr(copy, method)()
+
+    each(sec >= 1, near_copies, "start")
+    each(up, rim_copies[0], "start")
 
     def fill(condition, ref, *index):
         @pl.when(condition)
@@ -248,7 +259,6 @@
     fine_rows, fine_cols = fine_mask_ref.shape[1:]
     coarse_rows, coarse_cols = coarse_mask_ref.shape[1:]
     count = (fine_rows * fine_cols + coarse_rows * coarse_cols) // 4
-    fine_groups = fine_rows * fine_cols // 4
     (
         first_ref,
         fine_high_ref,
@@ -279,7 +289,7 @@
     scales = []
 
     def analyse(section, main_ref):
-        pl.when(below & (sec + section < secs))(rim_copies[section].wait_recv)
+        each(below & (sec + section < secs), rim_copies[section], "wait_recv")
         weight = jnp.concatenate([weight_ref[...]] * 2, axis=1)
         real, imag = section_spectra(
             jnp.concatenate([main_ref[...], rim_ref[section]], axis=0),
@@ -312,33 +322,52 @@
         maps = matmul(last_ref[...], jnp.concatenate([high, low, high], axis=0))
         for g in range(count):
             scale = scales[0][g : g + 1] * scales[d][g : g + 1] * masks[g] * (1.0 / float(PATCH) ** 3)
-            value = block_transpose(maps[:, LANES * g : LANES * (g + 1)] * scale)
+            maps_ref[d - 1, g] = maps[:, LANES * g : LANES * (g + 1)] * scale
+
+    @pl.when(has_near)
+    def _():
+        for c in range(CHUNKS):
+            near_copies[c].wait_recv()
+            pl.when(sec >= 1)(far_copies[c].start)
+            pl.when(up)(rim_copies[1][c].start)
+
+    own_copy.wait()
+    for copy in const_copies:
+        copy.wait()
+    analyse(0, own_ref)
+
+    @pl.when(has_far)
+    def _():
+        for c in range(CHUNKS):
+            far_copies[c].wait_recv()
+            pl.when(up)(rim_copies[2][c].start)
+
+    analyse(1, near_ref)
+    correlate(1)
+    analyse(2, far_ref)
+    correlate(2)
+    each(sec >= 1, near_copies, "wait_send")
+    each(has_near & (sec >= 1), far_copies, "wait_send")
+    each(up, rim_copies[0], "wait_send")
+    each(has_near & up, rim_copies[1], "wait_send")
+    each(has_far & up, rim_copies[2], "wait_send")
+
+
+def arrange(maps_ref, fine_out_ref, coarse_out_ref):
+    fine_rows, fine_cols = fine_out_ref.shape[2:4]
+    coarse_rows, coarse_cols = coarse_out_ref.shape[2:4]
+    fine_groups = fine_rows * fine_cols // 4
+    count = fine_groups + coarse_rows * coarse_cols // 4
+    for d in range(2):
+        for g in range(count):
+            value = block_transpose(maps_ref[d, g])
             if g < fine_groups:
                 ref, local_g, cols = fine_out_ref, g, fine_cols
             else:
                 ref, local_g, cols = coarse_out_ref, g - fine_groups, coarse_cols
             i, j = divmod(4 * local_g, cols)
             for q in range(WINDOW // 4):
-                ref[0, d - 1, i, j : j + 4, LANES * q : LANES * (q + 1)] = value[4 * q : 4 * (q + 1)]
-
-    own_copy.wait()
-    for copy in const_copies:
-        copy.wait()
-    has_near, has_far = sec + 1 < secs, sec + 2 < secs
-    pl.when(has_near)(near_copy.wait_recv)
-    pl.when(has_near & up)(rim_copies[1].start)
-    analyse(0, own_ref)
-    pl.when(has_far)(far_copy.wait_recv)
-    pl.when(has_far & up)(rim_copies[2].start)
-    analyse(1, near_ref)
-    correlate(1)
-    analyse(2, far_ref)
-    correlate(2)
-    pl.when(sec >= 2)(far_copy.wait_send)
-    pl.when(sec >= 1)(near_copy.wait_send)
-    pl.when(up)(rim_copies[0].wait_send)
-    pl.when(has_near & up)(rim_copies[1].wait_send)
-    pl.when(has_far & up)(rim_copies[2].wait_send)
+                ref[0, d, i, j : j + 4, LANES * q : LANES * (q + 1)] = value[4 * q : 4 * (q + 1)]
 
 
 def local(sections, mask_fine, mask_coarse):
@@ -350,14 +379,11 @@
     vmem = pl.BlockSpec(memory_space=pltpu.VMEM)
     anywhere = pl.BlockSpec(memory_space=pl.ANY)
     flat = WINDOW * WINDOW
-    return pl.pallas_call(
+    maps = pl.pallas_call(
         functools.partial(compute, len(consts)),
-        out_shape=(
-            jax.ShapeDtypeStruct((1, 2, fine_rows, fine_cols, flat), F32),
-            jax.ShapeDtypeStruct((1, 2, coarse_rows, coarse_cols, flat), F32),
-        ),
+        out_shape=jax.ShapeDtypeStruct((2, count, WINDOW, LANES), F32),
         in_specs=[anywhere, vmem, vmem] + [anywhere] * len(consts),
-        out_specs=(vmem, vmem),
+        out_specs=vmem,
         scratch_shapes=[
             pltpu.VMEM((strip_rows, width), BF16),
             pltpu.VMEM((strip_rows, width), BF16),
@@ -369,11 +395,20 @@
             *[pltpu.VMEM(c.shape, c.dtype) for c in consts],
             pltpu.SemaphoreType.DMA,
             pltpu.SemaphoreType.DMA((len(consts),)),
-            pltpu.SemaphoreType.DMA((5,)),
-            pltpu.SemaphoreType.DMA((5,)),
+            pltpu.SemaphoreType.DMA((5, CHUNKS)),
+            pltpu.SemaphoreType.DMA((5, CHUNKS)),
         ],
         compiler_params=pltpu.CompilerParams(collective_id=0, has_side_effects=True),
     )(sections, mask_fine, mask_coarse, *consts)
+    return pl.pallas_call(
+        arrange,
+        out_shape=(
+            jax.ShapeDtypeStruct((1, 2, fine_rows, fine_cols, flat), F32),
+            jax.ShapeDtypeStruct((1, 2, coarse_rows, coarse_cols, flat), F32),
+        ),
+        in_specs=[vmem],
+        out_specs=(vmem, vmem),
+    )(maps)
 
 
 def solution(mesh):

time: 19.6 us -> 19.1 us (0.974)
  the two profiles are of different devices: /device:TPU:9 before, /device:TPU:1 now
where the time goes in v2:
time: 19.1 us; the launch traced here: 18.9 us
  Pallas kernels  18.3 us (96%)
  between operations  0.64 us (3%)
    pallas_call x1, Pallas kernels, local(): pl.pallas_call(functools.partial(compute, len(consts)), out_shape=jax.Sha...  15.7 us
    pallas_call x1, Pallas kernels, local(): pl.pallas_call(arrange, out_shape=(jax.ShapeDtypeStruct((1, 2, fine_rows,...  2.63 us

profile of v2, /device:TPU:1, one launch (start us, length us, event | category | flops | bytes accessed | tf_op | source)
XLA Modules:
  0.0 18.9 jit_solution(16373658041850697964)
XLA Ops:
  0.6 15.7 %shard_map.140.maps_ref = f32[2,10,32,128]{3,2,1,0:T(8,128)} custom-call(bf16[1,64,512]{2,1,0:T(8,128)(2,1)} %refs_0_.1, s32[1,2,16]{2,1,0:T(2,128)} %refs_1_.1, s32[1,1,8]{2,1,0:T(1,128)} %refs_2_.1, bf16[240,256]{1,0:T(8,128)(2,1)} %constant.20.clone.refs_3_, bf16[256,512]{1,0:T(8,128)(2,1)} %constant.21.clone.refs_4_, ...), custom_call_target="tpu_custom_call" | custom-call | tf_op jit(solution)/shard_map/pallas_call | solution.py:382
  16.3 2.6 %shard_map.141 = (f32[1,2,2,16,1024]{4,3,2,1,0:T(8,128)}, f32[1,2,1,8,1024]{4,3,2,1,0:T(8,128)}) custom-call(f32[2,10,32,128]{3,2,1,0:T(8,128)} %shard_map.140.maps_ref), custom_call_target="tpu_custom_call" | custom-call | tf_op jit(solution)/shard_map/pallas_call | solution.py:403

commit v3 on v2

--- a/solution.py
+++ b/solution.py
@@ -13,7 +13,7 @@
 WINDOW = 32
 HALF = PATCH // 2 + 1
 KP = 40
-CHUNKS = 2
+CHUNKS = 4
 LANES = 128
 F32 = jnp.float32
 BF16 = jnp.bfloat16
@@ -242,8 +242,9 @@
             for copy in copies:
                 getattr(copy, method)()
 
-    each(sec >= 1, near_copies, "start")
-    each(up, rim_copies[0], "start")
+    for c in range(CHUNKS):
+        pl.when(up)(rim_copies[0][c].start)
+        pl.when(sec >= 1)(near_copies[c].start)
 
     def fill(condition, ref, *index):
         @pl.when(condition)
@@ -328,8 +329,8 @@
     def _():
         for c in range(CHUNKS):
             near_copies[c].wait_recv()
+            pl.when(up)(rim_copies[1][c].start)
             pl.when(sec >= 1)(far_copies[c].start)
-            pl.when(up)(rim_copies[1][c].start)
 
     own_copy.wait()
     for copy in const_copies:
@@ -358,7 +359,7 @@
     coarse_rows, coarse_cols = coarse_out_ref.shape[2:4]
     fine_groups = fine_rows * fine_cols // 4
     count = fine_groups + coarse_rows * coarse_cols // 4
-    for d in range(2):
+    for d in range(1):
         for g in range(count):
             value = block_transpose(maps_ref[d, g])
             if g < fine_groups:
@@ -406,8 +407,12 @@
             jax.ShapeDtypeStruct((1, 2, fine_rows, fine_cols, flat), F32),
             jax.ShapeDtypeStruct((1, 2, coarse_rows, coarse_cols, flat), F32),
         ),
-        in_specs=[vmem],
-        out_specs=(vmem, vmem),
+        grid=(2,),
+        in_specs=[pl.BlockSpec((1, count, WINDOW, LANES), lambda d: (d, 0, 0, 0))],
+        out_specs=(
+            pl.BlockSpec((1, 1, fine_rows, fine_cols, flat), lambda d: (0, d, 0, 0, 0)),
+            pl.BlockSpec((1, 1, coarse_rows, coarse_cols, flat), lambda d: (0, d, 0, 0, 0)),
+        ),
     )(maps)
 
 

time: 19.1 us -> 18.4 us (0.963)
  Pallas kernels: 18.3 us -> 17.6 us
    pallas_call x1, Pallas kernels: 2.63 us -> 2.04 us  [local(): pl.pallas_call(arrange, out_shape=(jax.ShapeDtypeStruct((1, 2, fine_rows,...]
where the time goes in v3:
time: 18.4 us; the launch traced here: 18.2 us
  Pallas kernels  17.6 us (96%)
  between operations  0.64 us (3%)
    pallas_call x1, Pallas kernels, local(): pl.pallas_call(functools.partial(compute, len(consts)), out_shape=jax.Sha...  15.5 us
    pallas_call x1, Pallas kernels, local(): pl.pallas_call(arrange, out_shape=(jax.ShapeDtypeStruct((1, 2, fine_rows,...  2.04 us

profile of v3, /device:TPU:1, one launch (start us, length us, event | category | flops | bytes accessed | tf_op | source)
XLA Modules:
  0.0 18.2 jit_solution(14207593237007501712)
XLA Ops:
  0.6 15.5 %shard_map.140.maps_ref = f32[2,10,32,128]{3,2,1,0:T(8,128)} custom-call(bf16[1,64,512]{2,1,0:T(8,128)(2,1)} %refs_0_.1, s32[1,2,16]{2,1,0:T(2,128)} %refs_1_.1, s32[1,1,8]{2,1,0:T(1,128)} %refs_2_.1, bf16[240,256]{1,0:T(8,128)(2,1)} %constant.20.clone.refs_3_, bf16[256,512]{1,0:T(8,128)(2,1)} %constant.21.clone.refs_4_, ...), custom_call_target="tpu_custom_call" | custom-call | tf_op jit(solution)/shard_map/pallas_call | solution.py:383
  16.1 2.0 %shard_map.141 = (f32[1,2,2,16,1024]{4,3,2,1,0:T(8,128)}, f32[1,2,1,8,1024]{4,3,2,1,0:T(8,128)}) custom-call(f32[2,10,32,128]{3,2,1,0:T(8,128)} %shard_map.140.maps_ref), custom_call_target="tpu_custom_call" | custom-call | tf_op jit(solution)/shard_map/pallas_call | solution.py:404

commit v4 on v3

--- a/solution.py
+++ b/solution.py
@@ -323,7 +323,7 @@
         maps = matmul(last_ref[...], jnp.concatenate([high, low, high], axis=0))
         for g in range(count):
             scale = scales[0][g : g + 1] * scales[d][g : g + 1] * masks[g] * (1.0 / float(PATCH) ** 3)
-            maps_ref[d - 1, g] = maps[:, LANES * g : LANES * (g + 1)] * scale
+            maps_ref[d - 1, g] = block_transpose(maps[:, LANES * g : LANES * (g + 1)] * scale)
 
     @pl.when(has_near)
     def _():
@@ -361,7 +361,7 @@
     count = fine_groups + coarse_rows * coarse_cols // 4
     for d in range(1):
         for g in range(count):
-            value = block_transpose(maps_ref[d, g])
+            value = maps_ref[d, g]
             if g < fine_groups:
                 ref, local_g, cols = fine_out_ref, g, fine_cols
             else:

time: 18.4 us -> 18.2 us (0.989)
  Pallas kernels: 17.6 us -> 17.4 us
    pallas_call x1, Pallas kernels: 2.04 us -> 1.69 us  [local(): pl.pallas_call(arrange, out_shape=(jax.ShapeDtypeStruct((1, 2, fine_rows,...]
where the time goes in v4:
time: 18.2 us; the launch traced here: 18 us
  Pallas kernels  17.4 us (96%)
  between operations  0.64 us (4%)
    pallas_call x1, Pallas kernels, local(): pl.pallas_call(functools.partial(compute, len(consts)), out_shape=jax.Sha...  15.7 us
    pallas_call x1, Pallas kernels, local(): pl.pallas_call(arrange, out_shape=(jax.ShapeDtypeStruct((1, 2, fine_rows,...  1.69 us

profile of v4, /device:TPU:1, one launch (start us, length us, event | category | flops | bytes accessed | tf_op | source)
XLA Modules:
  0.0 18.0 jit_solution(16734327367046390080)
XLA Ops:
  0.6 15.7 %shard_map.140.maps_ref = f32[2,10,32,128]{3,2,1,0:T(8,128)} custom-call(bf16[1,64,512]{2,1,0:T(8,128)(2,1)} %refs_0_.1, s32[1,2,16]{2,1,0:T(2,128)} %refs_1_.1, s32[1,1,8]{2,1,0:T(1,128)} %refs_2_.1, bf16[240,256]{1,0:T(8,128)(2,1)} %constant.20.clone.refs_3_, bf16[256,512]{1,0:T(8,128)(2,1)} %constant.21.clone.refs_4_, ...), custom_call_target="tpu_custom_call" | custom-call | tf_op jit(solution)/shard_map/pallas_call | solution.py:383
  16.3 1.7 %shard_map.141 = (f32[1,2,2,16,1024]{4,3,2,1,0:T(8,128)}, f32[1,2,1,8,1024]{4,3,2,1,0:T(8,128)}) custom-call(f32[2,10,32,128]{3,2,1,0:T(8,128)} %shard_map.140.maps_ref), custom_call_target="tpu_custom_call" | custom-call | tf_op jit(solution)/shard_map/pallas_call | solution.py:404
